TPU v7x, 32 devices: a whole 2x2x4 slice. The times are simulated.
32 devices in a mesh: groups: 2 (over x), head: 16 (over z, y, core).
Axes of the slice: x: 2, y: 2, z: 4, core: 2. Of those that a mesh axis runs over, the one named last changes fastest.
Arguments:
- queries: bfloat16 [256, 2048], P('groups', 'head'), parts along dimension 0, may hold values from -400 to 400
- cache: bfloat16 [2, 8192, 128], P(None, ('groups', 'head')), parts along dimension 1, may hold values from -5 to 5
- cache_scale: bfloat16 [2, 1, 8192], P(None, None, ('groups', 'head')), parts along dimension 2, may hold values from 0.5 to 4
- offsets: int32 [4], P('groups'), parts along dimension 0, may hold values from 0 to 2048, as said below
- lengths: int32 [4], P('groups'), parts along dimension 0, may hold values from 64 to 2048, as said below
- clamp_code: int32 [2], P('groups'), parts along dimension 0, may hold values from 512 to 1535
- w_out: bfloat16 [2048, 16384], P('head'), may hold values from -0.125 to 0.125
Outputs:
- projected: bfloat16 [16384, 256], P('head', 'groups'), parts along dimension 1
There are 2 independent parts, one for each index of `groups`. A program takes and returns all parts, laid end to end along the dimension named above; an argument that names none is the same for every part. Nothing has to cross between parts.
Inputs may be any that keep to these rules, and one draw needn't show every extreme that they name: Request r's cache region is offsets[r] to offsets[r] + lengths[r] - 1 and lies within positions r * 2048 to (r + 1) * 2048 - 1. `lengths`: the last 64 positions of each region hold the span's own keys and values; in every draw some request's length is exactly 2048.
All inputs are finite; a program needn't handle non-finite values.
Results may differ from a plain program's by a relative error of at most 0.0068.
Values may be sent and summed in bfloat16 or wider, within the bound.
No kernel may reach another device: no remote copies, remote signals or barrier semaphores. Data moves between devices by JAX's collectives and lax.ppermute only.
A program may use at most 128 MiB of HBM per device.

v0:
```python
import math
import jax
import jax.numpy as jnp
from jax import lax
from jax.sharding import PartitionSpec as P

SPAN = 64
NEG_FILL = -1e30


def hadamard(matrix_size):
    counter_index = jnp.arange(matrix_size, dtype=jnp.int32)
    common = counter_index[:, None] & counter_index[None, :]
    parity = jnp.zeros((matrix_size, matrix_size), jnp.int32)
    for bit_place in range(matrix_size.bit_length() - 1):
        parity = parity + (common >> bit_place & 1)
    return jnp.where(parity % 2 == 0, 1.0, -1.0).astype(jnp.float32)


def masked_scores(query_block, key_rows, key_scale, visible_tile, inv_root):
    scores = jnp.einsum("tjd,pd->jtp", query_block, key_rows, preferred_element_type=jnp.float32)
    scores = scores * (key_scale.astype(jnp.float32) * inv_root)[None, None, :]
    return jnp.where(visible_tile[None], scores, NEG_FILL)


def tile_sums(masked, row_max, visible_tile, value_scale, value_rows):
    weights = jnp.where(visible_tile[None], jnp.exp(masked - row_max[..., None]), 0.0)
    prob_rows = (weights * value_scale.astype(jnp.float32)[None, None, :]).astype(jnp.bfloat16)
    numerator = jnp.einsum("jtp,pd->jtd", prob_rows, value_rows, preferred_element_type=jnp.float32)
    return (numerator, jnp.sum(weights, axis=2))


def per_device(queries, cache, cache_scale, offsets, lengths, clamp_code, w_out):
    my_index = lax.axis_index("head")
    head_dim = queries.shape[1]
    local_len = cache.shape[1]
    kv_count = cache.shape[2] // head_dim
    gathered = lax.all_gather(queries, "head", axis=1, tiled=True)
    tok_rows = gathered.shape[0]
    head_count = gathered.shape[1] // head_dim
    per_group = head_count // kv_count
    token_ids = jnp.arange(tok_rows, dtype=jnp.int32)
    request = token_ids // SPAN
    within = token_ids % SPAN
    req_match = request[:, None] == jnp.arange(offsets.shape[0], dtype=jnp.int32)[None, :]
    starts = jnp.sum(jnp.where(req_match, offsets[None, :], 0), axis=1)
    last_pos = starts + jnp.sum(jnp.where(req_match, lengths[None, :], 0), axis=1) - SPAN + within
    inv_root = 1.0 / math.sqrt(head_dim)
    positions = my_index * local_len + jnp.arange(local_len, dtype=jnp.int32)
    visible = (positions[None, :] >= starts[:, None]) & (positions[None, :] <= last_pos[:, None])
    max_parts = []
    for kv_index in range(kv_count):
        column_left = kv_index * head_dim
        query_block = gathered[
            :, column_left * per_group : (column_left + head_dim) * per_group
        ].reshape(tok_rows, per_group, head_dim)
        masked = masked_scores(
            query_block,
            cache[0, :, column_left : column_left + head_dim],
            cache_scale[0, kv_index],
            visible,
            inv_root,
        )
        max_parts.append(jnp.max(masked, axis=2))
    local_max = jnp.concatenate(max_parts, 0)
    global_max = lax.pmax(local_max, "head")
    numer_parts = []
    denom_parts = []
    for kv_index in range(kv_count):
        column_left = kv_index * head_dim
        query_block = gathered[
            :, column_left * per_group : (column_left + head_dim) * per_group
        ].reshape(tok_rows, per_group, head_dim)
        masked = masked_scores(
            query_block,
            cache[0, :, column_left : column_left + head_dim],
            cache_scale[0, kv_index],
            visible,
            inv_root,
        )
        row_max = global_max[kv_index * per_group : (kv_index + 1) * per_group]
        numer_part, denom_part = tile_sums(
            masked,
            row_max,
            visible,
            cache_scale[1, kv_index],
            cache[1, :, column_left : column_left + head_dim],
        )
        numer_parts.append(numer_part)
        denom_parts.append(denom_part)
    numerator = jnp.concatenate(numer_parts, 0)
    denominator = jnp.concatenate(denom_parts, 0)
    numer_rows, denom_rows = (
        lax.psum_scatter(numerator, "head", scatter_dimension=1, tiled=True),
        lax.psum_scatter(denominator, "head", scatter_dimension=1, tiled=True),
    )
    token_attention = (numer_rows / denom_rows[..., None]).astype(jnp.bfloat16)
    clip_limit = clamp_code[0].astype(jnp.float32) / 1024.0
    scale_out = 1.0 / math.sqrt(head_count * head_dim)
    hd_matrix = hadamard(head_dim).astype(jnp.bfloat16)
    inner_mixed = jnp.einsum(
        "hrd,de->hre", token_attention, hd_matrix, preferred_element_type=jnp.float32
    )
    rotated = jnp.einsum(
        "gh,hre->gre", hadamard(head_count), inner_mixed, precision=lax.Precision.HIGHEST
    )
    clamped = jnp.clip(rotated * scale_out, -clip_limit, clip_limit).astype(jnp.bfloat16)
    activation = lax.all_to_all(clamped, "head", split_axis=0, concat_axis=1, tiled=True)[0]
    projected = lax.psum_scatter(
        lax.dot_general(
            w_out, activation, (((0,), (1,)), ((), ())), preferred_element_type=jnp.float32
        ),
        "head",
        scatter_dimension=0,
        tiled=True,
    )
    return projected.astype(jnp.bfloat16)


def solution(mesh):
    return jax.shard_map(
        per_device,
        mesh=mesh,
        in_specs=(
            P("groups", "head"),
            P(None, ("groups", "head"), None),
            P(None, None, ("groups", "head")),
            P("groups"),
            P("groups"),
            P("groups"),
            P("head", None),
        ),
        out_specs=P("head", "groups"),
        check_vma=False,
    )
```

profile of v0, /device:TPU:0, one launch (start us, length us, event | category | flops | bytes accessed | tf_op | source)
XLA Modules:
  0.0 251.2 jit_solution(6421445603097386101)
XLA Ops:
  6.5 0.0 copy-start
  6.5 0.0 reduce-scatter.4.cloned.1.call-start
  6.5 0.7 slice_convert_fusion
  7.3 0.7 convert_multiply_fusion
  7.9 0.9 copy.19
  8.8 24.6 %all_gather.3 = bf16[128,2048]{0,1:T(8,128)(2,1)S(1)} all-gather(bf16[128,128]{0,1:T(8,128)(2,1)S(1)} %copy.19), channel_id=1, replica_groups=mesh['groups'=2,'head'=16] {'head'}, dimensions={1}, use_global_device_ids=true | all-gather | bytes 557056 | tf_op jit(solution)/shard_map/all_gather | solution.py:38
  33.4 0.8 select_reduce_fusion
  34.2 0.1 compare_and_fusion
  34.3 1.3 fusion
  35.6 30.3 %pmax.7 = f32[16,128]{1,0:T(8,128)S(1)} all-reduce(f32[16,128]{1,0:T(8,128)S(1)} %get-tuple-element.7), channel_id=1, replica_groups=mesh['groups'=2,'head'=16] {'head'}, use_global_device_ids=true, to_apply=%region_3.4 | all-reduce | flops 2048 | bytes 16384 | tf_op jit(solution)/shard_map/pmax | solution.py:66
  65.9 0.0 copy-done
  65.9 0.0 copy-start.1
  66.0 1.9 fusion.5
  67.9 0.0 reduce-scatter.4.cloned.1.call-update
  67.9 0.0 reduce-scatter.6.cloned.1.call-start
  68.6 0.0 copy-done.1
  68.6 0.6 dynamic-slice
  69.9 0.6 fusion.1
  70.4 30.2 %all-reduce = f32[16,128]{1,0:T(8,128)S(1)} all-reduce(f32[16,128]{1,0:T(8,128)S(1)} %fusion.1), channel_id=3, replica_groups=mesh['groups'=2,'head'=16] {'head'}, use_global_device_ids=true, to_apply=%region_6.7.clone | all-reduce | flops 2048 | bytes 16384
  100.7 0.1 constant_dynamic-slice_fusion
  100.7 22.4 %reduce-scatter.4.cloned.1.call-done = f32[16,8,128]{2,1,0:T(8,128)} async-done(((f32[16,128,128]{2,1,0:T(8,128)}), f32[16,8,128]{2,1,0:T(8,128)}) %reduce-scatter.4.cloned.1.call-update) | async-done | bytes 65552 | tf_op jit(solution)/shard_map/reduce_scatter | solution.py:94
  123.1 0.9 divide_convert_fusion
  124.1 0.2 fusion.14
  124.3 0.2 fusion.4
  124.5 10.1 %all_to_all.4 = bf16[16,8,128]{2,1,0:T(8,128)(2,1)S(1)} all-to-all(bf16[16,8,128]{2,1,0:T(8,128)(2,1)S(1)} %copy.23), channel_id=1, replica_groups=mesh['groups'=2,'head'=16] {'head'}, dimensions={0} | all-to-all | bytes 65536 | tf_op jit(solution)/shard_map/all_to_all | solution.py:108
  134.6 6.7 %convolution_bitcast_fusion = f32[16384,128]{0,1:T(8,128)} fusion(bf16[128,16384]{1,0:T(8,128)(2,1)} %param.13, bf16[16,8,128]{2,1,0:T(8,128)(2,1)S(1)} %all_to_all.4), kind=kOutput, calls=%fused_computation | convolution fusion | flops 536870912 | bytes 12615680 | tf_op jit(solution)/shard_map/dot_general | solution.py:110
  141.3 0.0 reduce-scatter.6.cloned.1.call-update
  141.3 101.1 %reduce-scatter.6.cloned.1.call-done = f32[1024,128]{0,1:T(8,128)} async-done(((f32[16384,128]{0,1:T(8,128)}), f32[1024,128]{0,1:T(8,128)}) %reduce-scatter.6.cloned.1.call-update) | async-done | bytes 524304 | tf_op jit(solution)/shard_map/reduce_scatter | solution.py:109
  242.4 1.1 convert_element_type.32
  243.5 0.8 copy.24
  (4 shorter events, 0.0 us)
Async XLA Ops:
  6.5 59.4 %copy-start = (bf16[2,256,128]{2,1,0:T(8,128)(2,1)S(1)}, bf16[2,256,128]{2,1,0:T(8,128)(2,1)}, u32[]{:S(2)}) copy-start(bf16[2,256,128]{2,1,0:T(8,128)(2,1)} %param.8) | copy-start | bytes 393220
  6.5 116.6 %reduce-scatter.4.cloned.1.call-start = ((), (), s32[]{:S(2)}) async-start(), calls=%async_computation.3 | async-start | bytes 1114112 | tf_op jit(solution)/shard_map/reduce_scatter | solution.py:94
  65.9 2.7 %copy-start.1 = (u32[32]{0:T(128)S(1)}, u32[32]{0:T(128)}, u32[]{:S(2)}) copy-start(u32[32]{0:T(128)} %constant.97) | copy-start | bytes 388
  67.9 174.5 %reduce-scatter.6.cloned.1.call-start = ((), (), s32[]{:S(2)}) async-start(), calls=%async_computation.4 | async-start | bytes 8912896 | tf_op jit(solution)/shard_map/reduce_scatter | solution.py:109
Sparse Core Ops, SparseCore 0:
  68.0 55.0 reduce-scatter.3
  141.4 100.9 reduce-scatter.5
where the time goes:
time: 252 us; the launch traced here: 251 us
  waiting for transfers between devices  124 us (49%)
  blocking collectives  95.3 us (38%)
  between operations  14.8 us (6%)
  matrix products  10.3 us (4%)
  other arithmetic  4.83 us (2%)
    reduce_scatter x1, waiting for transfers between devices, per_device(): lax.psum_scatter(lax.dot_general(w_out, activation, (((0,), (1,)), ((), (...  101 us
    pmax x1, blocking collectives, per_device(): global_max = lax.pmax(local_max, 'head')  30.3 us
    unnamed x1, blocking collectives  30.2 us
    all_gather x1, blocking collectives, per_device(): gathered = lax.all_gather(queries, 'head', axis=1, tiled=True)  24.6 us
    reduce_scatter x1, waiting for transfers between devices, per_device(): lax.psum_scatter(numerator, 'head', scatter_dimension=1, tiled=True)  22.4 us
    all_to_all x1, blocking collectives, per_device(): lax.all_to_all(clamped, 'head', split_axis=0, concat_axis=1, tiled=True)[0]  10.1 us
    dot_general x1, matrix products, per_device(): lax.dot_general(w_out, activation, (((0,), (1,)), ((), ())), preferred_el...  6.66 us
  transfers between devices with their start and end apart: 2, of which 2 were waited for; matrix products, arithmetic and copies ran while one was open for 0% of the time, Pallas kernels for 0%

commit v1 on v0

--- a/solution.py
+++ b/solution.py
@@ -6,6 +6,16 @@
 
 SPAN = 64
 NEG_FILL = -1e30
+
+
+def pass_along(x, axis, d):
+    size = lax.axis_size(axis)
+    held, pieces = (x, [x])
+    for _ in range(size - 1):
+        held = lax.ppermute(held, axis, [(i, (i + 1) % size) for i in range(size)])
+        pieces.insert(0, held)
+    row_of_blocks = jnp.concatenate(pieces, axis=d)
+    return jnp.roll(row_of_blocks, (lax.axis_index(axis) + 1) * x.shape[d], axis=d)
 
 
 def hadamard(matrix_size):
@@ -35,7 +45,7 @@
     head_dim = queries.shape[1]
     local_len = cache.shape[1]
     kv_count = cache.shape[2] // head_dim
-    gathered = lax.all_gather(queries, "head", axis=1, tiled=True)
+    gathered = pass_along(queries, "head", 1)
     tok_rows = gathered.shape[0]
     head_count = gathered.shape[1] // head_dim
     per_group = head_count // kv_count

time: 252 us -> 316 us (1.25)
  waiting for transfers between devices: 124 us -> 212 us
  blocking collectives: 95.3 us -> 70.4 us
    ppermute x0 -> x15, waiting for transfers between devices: none -> 88.8 us  [pass_along(): held = lax.ppermute(held, axis, [(i, (i + 1) % size) for i in range(size)])]
    all_gather x1 -> x0, blocking collectives: 24.6 us -> none  [per_device(): gathered = lax.all_gather(queries, 'head', axis=1, tiled=True)]
  transfers between devices with their start and end apart: 2 -> 17, of which waited for: 2 -> 17; matrix products, arithmetic and copies ran while one was open for 0% -> 1% of each run, Pallas kernels for 0% -> 0%
where the time goes in v1:
time: 316 us
  waiting for transfers between devices  212 us (67%)
  blocking collectives  70.4 us (22%)
  between operations  15 us (5%)
  matrix products  9.38 us (3%)
  other arithmetic  5.08 us (2%)
    reduce_scatter x1, waiting for transfers between devices, per_device(): lax.psum_scatter(lax.dot_general(w_out, activation, (((0,), (1,)), ((), (...  101 us
    ppermute x15, waiting for transfers between devices, pass_along(): held = lax.ppermute(held, axis, [(i, (i + 1) % size) for i in range(size)])  88.8 us
    unnamed x1, blocking collectives  30.3 us
    pmax x1, blocking collectives, per_device(): global_max = lax.pmax(local_max, 'head')  30 us
    reduce_scatter x1, waiting for transfers between devices, per_device(): lax.psum_scatter(numerator, 'head', scatter_dimension=1, tiled=True)  22.5 us
    all_to_all x1, blocking collectives, per_device(): lax.all_to_all(clamped, 'head', split_axis=0, concat_axis=1, tiled=True)[0]  10.2 us
    dot_general x1, matrix products, per_device(): lax.dot_general(w_out, activation, (((0,), (1,)), ((), ())), preferred_el...  6.64 us
  transfers between devices with their start and end apart: 17, of which 17 were waited for; matrix products, arithmetic and copies ran while one was open for 1% of the time, Pallas kernels for 0%

profile of v1, /device:TPU:0, one launch (start us, length us, event | category | flops | bytes accessed | tf_op | source)
XLA Modules:
  0.0 315.7 jit_solution(4039181844055805137)
XLA Ops:
  6.5 0.9 copy.22
  8.0 6.6 %collective-permute-done = bf16[128,128]{0,1:T(8,128)(2,1)S(1)} collective-permute-done((bf16[128,128]{0,1:T(8,128)(2,1)S(1)}, bf16[128,128]{0,1:T(8,128)(2,1)S(1)}, u32[]{:S(2)}, u32[]{:S(2)}) %collective-permute-start) | collective-permute-done | bytes 32800 | tf_op jit(solution)/shard_map/ppermute | solution.py:15
  14.6 6.0 %collective-permute-done.1 = bf16[128,128]{0,1:T(8,128)(2,1)S(1)} collective-permute-done((bf16[128,128]{0,1:T(8,128)(2,1)S(1)}, bf16[128,128]{0,1:T(8,128)(2,1)S(1)}, u32[]{:S(2)}, u32[]{:S(2)}) %collective-permute-start.1) | collective-permute-done | bytes 32800 | tf_op jit(solution)/shard_map/ppermute | solution.py:15
  20.6 6.0 %collective-permute-done.2 = bf16[128,128]{0,1:T(8,128)(2,1)S(1)} collective-permute-done((bf16[128,128]{0,1:T(8,128)(2,1)S(1)}, bf16[128,128]{0,1:T(8,128)(2,1)S(1)}, u32[]{:S(2)}, u32[]{:S(2)}) %collective-permute-start.2) | collective-permute-done | bytes 32800 | tf_op jit(solution)/shard_map/ppermute | solution.py:15
  26.6 6.0 %collective-permute-done.3 = bf16[128,128]{0,1:T(8,128)(2,1)S(1)} collective-permute-done((bf16[128,128]{0,1:T(8,128)(2,1)S(1)}, bf16[128,128]{0,1:T(8,128)(2,1)S(1)}, u32[]{:S(2)}, u32[]{:S(2)}) %collective-permute-start.3) | collective-permute-done | bytes 32800 | tf_op jit(solution)/shard_map/ppermute | solution.py:15
  32.7 6.0 %collective-permute-done.4 = bf16[128,128]{0,1:T(8,128)(2,1)S(1)} collective-permute-done((bf16[128,128]{0,1:T(8,128)(2,1)S(1)}, bf16[128,128]{0,1:T(8,128)(2,1)S(1)}, u32[]{:S(2)}, u32[]{:S(2)}) %collective-permute-start.4) | collective-permute-done | bytes 32800 | tf_op jit(solution)/shard_map/ppermute | solution.py:15
  38.7 6.0 %collective-permute-done.5 = bf16[128,128]{0,1:T(8,128)(2,1)S(1)} collective-permute-done((bf16[128,128]{0,1:T(8,128)(2,1)S(1)}, bf16[128,128]{0,1:T(8,128)(2,1)S(1)}, u32[]{:S(2)}, u32[]{:S(2)}) %collective-permute-start.5) | collective-permute-done | bytes 32800 | tf_op jit(solution)/shard_map/ppermute | solution.py:15
  44.8 6.0 %collective-permute-done.6 = bf16[128,128]{0,1:T(8,128)(2,1)S(1)} collective-permute-done((bf16[128,128]{0,1:T(8,128)(2,1)S(1)}, bf16[128,128]{0,1:T(8,128)(2,1)S(1)}, u32[]{:S(2)}, u32[]{:S(2)}) %collective-permute-start.6) | collective-permute-done | bytes 32800 | tf_op jit(solution)/shard_map/ppermute | solution.py:15
  50.8 6.0 %collective-permute-done.7 = bf16[128,128]{0,1:T(8,128)(2,1)S(1)} collective-permute-done((bf16[128,128]{0,1:T(8,128)(2,1)S(1)}, bf16[128,128]{0,1:T(8,128)(2,1)S(1)}, u32[]{:S(2)}, u32[]{:S(2)}) %collective-permute-start.7) | collective-permute-done | bytes 32800 | tf_op jit(solution)/shard_map/ppermute | solution.py:15
  56.8 6.0 %collective-permute-done.8 = bf16[128,128]{0,1:T(8,128)(2,1)S(1)} collective-permute-done((bf16[128,128]{0,1:T(8,128)(2,1)S(1)}, bf16[128,128]{0,1:T(8,128)(2,1)S(1)}, u32[]{:S(2)}, u32[]{:S(2)}) %collective-permute-start.8) | collective-permute-done | bytes 32800 | tf_op jit(solution)/shard_map/ppermute | solution.py:15
  62.9 0.8 select_reduce_fusion
  63.6 5.3 %collective-permute-done.9 = bf16[128,128]{0,1:T(8,128)(2,1)S(1)} collective-permute-done((bf16[128,128]{0,1:T(8,128)(2,1)S(1)}, bf16[128,128]{0,1:T(8,128)(2,1)S(1)}, u32[]{:S(2)}, u32[]{:S(2)}) %collective-permute-start.9) | collective-permute-done | bytes 32800 | tf_op jit(solution)/shard_map/ppermute | solution.py:15
  68.9 6.0 %collective-permute-done.10 = bf16[128,128]{0,1:T(8,128)(2,1)S(1)} collective-permute-done((bf16[128,128]{0,1:T(8,128)(2,1)S(1)}, bf16[128,128]{0,1:T(8,128)(2,1)S(1)}, u32[]{:S(2)}, u32[]{:S(2)}) %collective-permute-start.10) | collective-permute-done | bytes 32800 | tf_op jit(solution)/shard_map/ppermute | solution.py:15
  74.9 6.0 %collective-permute-done.11 = bf16[128,128]{0,1:T(8,128)(2,1)S(1)} collective-permute-done((bf16[128,128]{0,1:T(8,128)(2,1)S(1)}, bf16[128,128]{0,1:T(8,128)(2,1)S(1)}, u32[]{:S(2)}, u32[]{:S(2)}) %collective-permute-start.11) | collective-permute-done | bytes 32800 | tf_op jit(solution)/shard_map/ppermute | solution.py:15
  81.1 5.9 %collective-permute-done.12 = bf16[128,128]{0,1:T(8,128)(2,1)S(1)} collective-permute-done((bf16[128,128]{0,1:T(8,128)(2,1)S(1)}, bf16[128,128]{0,1:T(8,128)(2,1)S(1)}, u32[]{:S(2)}, u32[]{:S(2)}) %collective-permute-start.12) | collective-permute-done | bytes 32800 | tf_op jit(solution)/shard_map/ppermute | solution.py:15
  87.0 0.7 slice_convert_fusion
  87.7 5.3 %collective-permute-done.13 = bf16[128,128]{0,1:T(8,128)(2,1)S(1)} collective-permute-done((bf16[128,128]{0,1:T(8,128)(2,1)S(1)}, bf16[128,128]{0,1:T(8,128)(2,1)S(1)}, u32[]{:S(2)}, u32[]{:S(2)}) %collective-permute-start.13) | collective-permute-done | bytes 32800 | tf_op jit(solution)/shard_map/ppermute | solution.py:15
  93.1 0.7 convert_multiply_fusion
  93.7 5.4 %collective-permute-done.14 = bf16[128,128]{0,1:T(8,128)(2,1)S(1)} collective-permute-done((bf16[128,128]{0,1:T(8,128)(2,1)S(1)}, bf16[128,128]{0,1:T(8,128)(2,1)S(1)}, u32[]{:S(2)}, u32[]{:S(2)}) %collective-permute-start.14) | collective-permute-done | bytes 32800 | tf_op jit(solution)/shard_map/ppermute | solution.py:15
  99.6 0.6 bitcast_reduce_fusion
  100.2 30.0 %pmax.7 = f32[16,128]{1,0:T(8,128)S(1)} all-reduce(f32[16,128]{1,0:T(8,128)S(1)} %get-tuple-element.7), channel_id=1, replica_groups=mesh['groups'=2,'head'=16] {'head'}, use_global_device_ids=true, to_apply=%region_3.4 | all-reduce | flops 2048 | bytes 16384 | tf_op jit(solution)/shard_map/pmax | solution.py:76
  130.2 1.7 fusion.6
  132.7 0.6 dynamic-slice
  133.9 0.8 fusion.2
  134.8 30.3 %all-reduce = f32[16,128]{1,0:T(8,128)S(1)} all-reduce(f32[16,128]{1,0:T(8,128)S(1)} %fusion.2), channel_id=3, replica_groups=mesh['groups'=2,'head'=16] {'head'}, use_global_device_ids=true, to_apply=%region_6.7.clone | all-reduce | flops 2048 | bytes 16384
  165.1 22.5 %reduce-scatter.4.cloned.1.call-done = f32[16,8,128]{2,1,0:T(8,128)} async-done(((f32[16,128,128]{2,1,0:T(8,128)}), f32[16,8,128]{2,1,0:T(8,128)}) %reduce-scatter.4.cloned.1.call-update) | async-done | bytes 65552 | tf_op jit(solution)/shard_map/reduce_scatter | solution.py:104
  187.6 0.9 divide_convert_fusion
  189.0 10.2 %all_to_all.4 = bf16[16,8,128]{2,1,0:T(8,128)(2,1)S(1)} all-to-all(bf16[16,8,128]{2,1,0:T(8,128)(2,1)S(1)} %copy.27), channel_id=1, replica_groups=mesh['groups'=2,'head'=16] {'head'}, dimensions={0} | all-to-all | bytes 65536 | tf_op jit(solution)/shard_map/all_to_all | solution.py:118
  199.1 6.6 %convolution_bitcast_fusion = f32[16384,128]{0,1:T(8,128)} fusion(bf16[128,16384]{1,0:T(8,128)(2,1)} %param.13, bf16[16,8,128]{2,1,0:T(8,128)(2,1)S(1)} %all_to_all.4), kind=kOutput, calls=%fused_computation | convolution fusion | flops 536870912 | bytes 12615680 | tf_op jit(solution)/shard_map/dot_general | solution.py:120
  205.8 101.1 %reduce-scatter.6.cloned.1.call-done = f32[1024,128]{0,1:T(8,128)} async-done(((f32[16384,128]{0,1:T(8,128)}), f32[1024,128]{0,1:T(8,128)}) %reduce-scatter.6.cloned.1.call-update) | async-done | bytes 524304 | tf_op jit(solution)/shard_map/reduce_scatter | solution.py:119
  306.9 1.1 convert_element_type.32
  308.0 0.8 copy.28
  (64 shorter events, 1.7 us)
Async XLA Ops:
  6.5 93.1 %copy-start = (bf16[2,256,128]{2,1,0:T(8,128)(2,1)S(1)}, bf16[2,256,128]{2,1,0:T(8,128)(2,1)}, u32[]{:S(2)}) copy-start(bf16[2,256,128]{2,1,0:T(8,128)(2,1)} %param.8) | copy-start | bytes 393220
  6.5 181.1 %reduce-scatter.4.cloned.1.call-start = ((), (), s32[]{:S(2)}) async-start(), calls=%async_computation.3 | async-start | bytes 1114112 | tf_op jit(solution)/shard_map/reduce_scatter | solution.py:104
  7.4 7.1 %collective-permute-start = (bf16[128,128]{0,1:T(8,128)(2,1)S(1)}, bf16[128,128]{0,1:T(8,128)(2,1)S(1)}, u32[]{:S(2)}, u32[]{:S(2)}) collective-permute-start(bf16[128,128]{0,1:T(8,128)(2,1)S(1)} %copy.22), channel_id=1, source_target_pairs={{0,1},{1,2},{2,3},{3,4},{4,5},{5,6},{6,7},{7,8},{8,9},{9,10},{10,1... | collective-permute-start | bytes 98312 | tf_op jit(solution)/shard_map/ppermute | solution.py:15
  14.6 6.0 %collective-permute-start.1 = (bf16[128,128]{0,1:T(8,128)(2,1)S(1)}, bf16[128,128]{0,1:T(8,128)(2,1)S(1)}, u32[]{:S(2)}, u32[]{:S(2)}) collective-permute-start(bf16[128,128]{0,1:T(8,128)(2,1)S(1)} %collective-permute-done), channel_id=1, source_target_pairs={{0,1},{1,2},{2,3},{3,4},{4,5},{5,6},{6,7},{7,8},{8,9},{9,10},{10,1... | collective-permute-start | bytes 98312 | tf_op jit(solution)/shard_map/ppermute | solution.py:15
  20.6 6.0 %collective-permute-start.2 = (bf16[128,128]{0,1:T(8,128)(2,1)S(1)}, bf16[128,128]{0,1:T(8,128)(2,1)S(1)}, u32[]{:S(2)}, u32[]{:S(2)}) collective-permute-start(bf16[128,128]{0,1:T(8,128)(2,1)S(1)} %collective-permute-done.1), channel_id=1, source_target_pairs={{0,1},{1,2},{2,3},{3,4},{4,5},{5,6},{6,7},{7,8},{8,9},{9,10},{10,1... | collective-permute-start | bytes 98312 | tf_op jit(solution)/shard_map/ppermute | solution.py:15
  26.6 6.0 %collective-permute-start.3 = (bf16[128,128]{0,1:T(8,128)(2,1)S(1)}, bf16[128,128]{0,1:T(8,128)(2,1)S(1)}, u32[]{:S(2)}, u32[]{:S(2)}) collective-permute-start(bf16[128,128]{0,1:T(8,128)(2,1)S(1)} %collective-permute-done.2), channel_id=1, source_target_pairs={{0,1},{1,2},{2,3},{3,4},{4,5},{5,6},{6,7},{7,8},{8,9},{9,10},{10,1... | collective-permute-start | bytes 98312 | tf_op jit(solution)/shard_map/ppermute | solution.py:15
  32.7 6.0 %collective-permute-start.4 = (bf16[128,128]{0,1:T(8,128)(2,1)S(1)}, bf16[128,128]{0,1:T(8,128)(2,1)S(1)}, u32[]{:S(2)}, u32[]{:S(2)}) collective-permute-start(bf16[128,128]{0,1:T(8,128)(2,1)S(1)} %collective-permute-done.3), channel_id=1, source_target_pairs={{0,1},{1,2},{2,3},{3,4},{4,5},{5,6},{6,7},{7,8},{8,9},{9,10},{10,1... | collective-permute-start | bytes 98312 | tf_op jit(solution)/shard_map/ppermute | solution.py:15
  38.7 6.0 %collective-permute-start.5 = (bf16[128,128]{0,1:T(8,128)(2,1)S(1)}, bf16[128,128]{0,1:T(8,128)(2,1)S(1)}, u32[]{:S(2)}, u32[]{:S(2)}) collective-permute-start(bf16[128,128]{0,1:T(8,128)(2,1)S(1)} %collective-permute-done.4), channel_id=1, source_target_pairs={{0,1},{1,2},{2,3},{3,4},{4,5},{5,6},{6,7},{7,8},{8,9},{9,10},{10,1... | collective-permute-start | bytes 98312 | tf_op jit(solution)/shard_map/ppermute | solution.py:15
  44.8 6.0 %collective-permute-start.6 = (bf16[128,128]{0,1:T(8,128)(2,1)S(1)}, bf16[128,128]{0,1:T(8,128)(2,1)S(1)}, u32[]{:S(2)}, u32[]{:S(2)}) collective-permute-start(bf16[128,128]{0,1:T(8,128)(2,1)S(1)} %collective-permute-done.5), channel_id=1, source_target_pairs={{0,1},{1,2},{2,3},{3,4},{4,5},{5,6},{6,7},{7,8},{8,9},{9,10},{10,1... | collective-permute-start | bytes 98312 | tf_op jit(solution)/shard_map/ppermute | solution.py:15
  50.8 6.0 %collective-permute-start.7 = (bf16[128,128]{0,1:T(8,128)(2,1)S(1)}, bf16[128,128]{0,1:T(8,128)(2,1)S(1)}, u32[]{:S(2)}, u32[]{:S(2)}) collective-permute-start(bf16[128,128]{0,1:T(8,128)(2,1)S(1)} %collective-permute-done.6), channel_id=1, source_target_pairs={{0,1},{1,2},{2,3},{3,4},{4,5},{5,6},{6,7},{7,8},{8,9},{9,10},{10,1... | collective-permute-start | bytes 98312 | tf_op jit(solution)/shard_map/ppermute | solution.py:15
  56.8 6.0 %collective-permute-start.8 = (bf16[128,128]{0,1:T(8,128)(2,1)S(1)}, bf16[128,128]{0,1:T(8,128)(2,1)S(1)}, u32[]{:S(2)}, u32[]{:S(2)}) collective-permute-start(bf16[128,128]{0,1:T(8,128)(2,1)S(1)} %collective-permute-done.7), channel_id=1, source_target_pairs={{0,1},{1,2},{2,3},{3,4},{4,5},{5,6},{6,7},{7,8},{8,9},{9,10},{10,1... | collective-permute-start | bytes 98312 | tf_op jit(solution)/shard_map/ppermute | solution.py:15
  62.9 6.0 %collective-permute-start.9 = (bf16[128,128]{0,1:T(8,128)(2,1)S(1)}, bf16[128,128]{0,1:T(8,128)(2,1)S(1)}, u32[]{:S(2)}, u32[]{:S(2)}) collective-permute-start(bf16[128,128]{0,1:T(8,128)(2,1)S(1)} %collective-permute-done.8), channel_id=1, source_target_pairs={{0,1},{1,2},{2,3},{3,4},{4,5},{5,6},{6,7},{7,8},{8,9},{9,10},{10,1... | collective-permute-start | bytes 98312 | tf_op jit(solution)/shard_map/ppermute | solution.py:15
  68.9 6.0 %collective-permute-start.10 = (bf16[128,128]{0,1:T(8,128)(2,1)S(1)}, bf16[128,128]{0,1:T(8,128)(2,1)S(1)}, u32[]{:S(2)}, u32[]{:S(2)}) collective-permute-start(bf16[128,128]{0,1:T(8,128)(2,1)S(1)} %collective-permute-done.9), channel_id=1, source_target_pairs={{0,1},{1,2},{2,3},{3,4},{4,5},{5,6},{6,7},{7,8},{8,9},{9,10},{10,1... | collective-permute-start | bytes 98312 | tf_op jit(solution)/shard_map/ppermute | solution.py:15
  74.9 6.0 %collective-permute-start.11 = (bf16[128,128]{0,1:T(8,128)(2,1)S(1)}, bf16[128,128]{0,1:T(8,128)(2,1)S(1)}, u32[]{:S(2)}, u32[]{:S(2)}) collective-permute-start(bf16[128,128]{0,1:T(8,128)(2,1)S(1)} %collective-permute-done.10), channel_id=1, source_target_pairs={{0,1},{1,2},{2,3},{3,4},{4,5},{5,6},{6,7},{7,8},{8,9},{9,10},{10,1... | collective-permute-start | bytes 98312 | tf_op jit(solution)/shard_map/ppermute | solution.py:15
  81.0 6.0 %collective-permute-start.12 = (bf16[128,128]{0,1:T(8,128)(2,1)S(1)}, bf16[128,128]{0,1:T(8,128)(2,1)S(1)}, u32[]{:S(2)}, u32[]{:S(2)}) collective-permute-start(bf16[128,128]{0,1:T(8,128)(2,1)S(1)} %collective-permute-done.11), channel_id=1, source_target_pairs={{0,1},{1,2},{2,3},{3,4},{4,5},{5,6},{6,7},{7,8},{8,9},{9,10},{10,1... | collective-permute-start | bytes 98312 | tf_op jit(solution)/shard_map/ppermute | solution.py:15
  87.0 6.0 %collective-permute-start.13 = (bf16[128,128]{0,1:T(8,128)(2,1)S(1)}, bf16[128,128]{0,1:T(8,128)(2,1)S(1)}, u32[]{:S(2)}, u32[]{:S(2)}) collective-permute-start(bf16[128,128]{0,1:T(8,128)(2,1)S(1)} %collective-permute-done.12), channel_id=1, source_target_pairs={{0,1},{1,2},{2,3},{3,4},{4,5},{5,6},{6,7},{7,8},{8,9},{9,10},{10,1... | collective-permute-start | bytes 98312 | tf_op jit(solution)/shard_map/ppermute | solution.py:15
  93.1 6.0 %collective-permute-start.14 = (bf16[128,128]{0,1:T(8,128)(2,1)S(1)}, bf16[128,128]{0,1:T(8,128)(2,1)S(1)}, u32[]{:S(2)}, u32[]{:S(2)}) collective-permute-start(bf16[128,128]{0,1:T(8,128)(2,1)S(1)} %collective-permute-done.13), channel_id=1, source_target_pairs={{0,1},{1,2},{2,3},{3,4},{4,5},{5,6},{6,7},{7,8},{8,9},{9,10},{10,1... | collective-permute-start | bytes 98312 | tf_op jit(solution)/shard_map/ppermute | solution.py:15
  130.2 2.5 copy-start.1
  132.0 174.9 %reduce-scatter.6.cloned.1.call-start = ((), (), s32[]{:S(2)}) async-start(), calls=%async_computation.4 | async-start | bytes 8912896 | tf_op jit(solution)/shard_map/reduce_scatter | solution.py:119
Sparse Core Ops, SparseCore 0:
  132.1 55.4 reduce-scatter.3
  205.9 100.9 reduce-scatter.5
